TPU v7x, 128 devices: a whole 4x4x4 slice. The times are simulated.
128 devices in a mesh: dp: 2 (over z_hi), seq: 32 (over y, x, core), tensor: 2 (over z_lo).
Axes of the slice: x: 4, y: 4, z: 4 (z_hi: 2, z_lo: 2; z = z_hi * 2 + z_lo), core: 2. Of those that a mesh axis runs over, the one named last changes fastest.
Arguments:
- queries: bfloat16 [2, 16384, 4096], P('dp', 'seq', 'tensor'), may hold values from -6 to 6
- keys: bfloat16 [2, 16384, 4096], P('dp', 'seq', 'tensor'), may hold values from -6 to 6
- values: bfloat16 [2, 16384, 4096], P('dp', 'seq', 'tensor'), may hold values from -40 to 40
- grad_out: bfloat16 [2, 16384, 4096], P('dp', 'seq', 'tensor'), may hold values from -48 to 48
- doc_lengths: int32 [2, 16], P('dp'), may hold values from 1 to 9216, 16384 in all within a row
- gain: float32 [4096], P('tensor'), may hold values from 0.1 to 1.9
Outputs:
- layer_out: bfloat16 [2, 16384, 4096], P('dp', 'seq', 'tensor')
- grad_queries: bfloat16 [2, 16384, 4096], P('dp', 'seq', 'tensor')
- grad_keys: bfloat16 [2, 16384, 4096], P('dp', 'seq', 'tensor')
- grad_values: bfloat16 [2, 16384, 4096], P('dp', 'seq', 'tensor')
- grad_gain: float32 [4096], P('tensor')
Inputs may be any that keep to these rules, and one draw needn't show every extreme that they name: `doc_lengths`: each row sums to 16384; in every sequence the longest document has exactly 9216 tokens.
All inputs are finite; a program needn't handle non-finite values.
Results may differ from a plain program's by a relative error of at most 0.0063.
Values may be sent and summed in bfloat16 or wider, within the bound.
No kernel may reach another device: no remote copies, remote signals or barrier semaphores. Data moves between devices by JAX's collectives and lax.ppermute only.
A program may use at most 128 MiB of HBM per device.

v0:
```python
import jax
import jax.numpy as jnp
from jax import lax
from jax.sharding import PartitionSpec as P

HEADS = 32
HD = 128
epsilon = 1e-05


def prefix(value, axis, join, neutral, backward):
    count = lax.axis_size(axis)
    place = lax.axis_index(axis)
    ahead = count - 1 - place if backward else place
    gathered = jax.tree.map(
        lambda a, kind: lax.all_gather(a.astype(kind), axis), value, (jnp.bfloat16, jnp.bfloat16)
    )
    state = jax.tree.map(lambda a, e: jnp.zeros_like(a) + jnp.asarray(e, a.dtype), value, neutral)

    def one(step, state):
        source = count - 1 - step if backward else step
        return join(
            state,
            jax.tree.map(
                lambda a, own: lax.dynamic_index_in_dim(a, source, 0, False).astype(own.dtype),
                gathered,
                value,
            ),
        )

    return lax.fori_loop(0, ahead, one, state)


def linked(earlier, later):
    keeping = 1.0 - later[1][0]
    return (later[0] + keeping * earlier[0], jnp.maximum(earlier[1], later[1]))


def carried(state, flags, backward):
    blank = jnp.zeros(state.shape, jnp.float32)
    total, unused = prefix(
        (state.astype(jnp.float32), flags),
        "seq",
        linked,
        (blank, jnp.zeros((1,), jnp.float32)),
        backward,
    )
    return total


def head_major(array, shape):
    return jnp.transpose(array.reshape(shape), (1, 0, 2))


def body(queries, keys, values, grad_out, doc_lengths, gain):
    count = queries.shape[1]
    local_width = queries.shape[2]
    local_heads = local_width // HD
    shape = (count, local_heads, HD)
    query = head_major(queries[0], shape)
    key = head_major(keys[0], shape)
    value = head_major(values[0], shape)
    lengths = doc_lengths[0]
    starts = jnp.cumsum(lengths) - lengths
    block = lax.axis_index("seq")
    begin = block * count
    position = begin + jnp.arange(count, dtype=jnp.int32)
    document = jnp.sum((starts[None, :] <= position[:, None]).astype(jnp.int32), axis=1) - 1
    first_doc = document[0]
    last_doc = document[-1]
    numbers = jnp.arange(starts.shape[0], dtype=jnp.int32)
    last_end = jnp.sum(jnp.where(numbers == last_doc, starts + lengths, 0))
    last_block = (last_end - 1) // count
    continues = jnp.logical_not(jnp.any(starts == begin))
    starts_here = jnp.any((starts >= begin) & (starts < begin + count))
    flags = starts_here.astype(jnp.float32).reshape(1)
    first_mask = (document == first_doc) & continues
    last_mask = document == last_doc
    indices = jnp.arange(count, dtype=jnp.int32)
    same = (indices[:, None] >= indices[None, :]) & (document[:, None] == document[None, :])
    key_last = jnp.where(last_mask[None, :, None], key, 0)
    value_last = jnp.where(last_mask[None, :, None], value, 0)
    query_first = jnp.where(first_mask[None, :, None], query, 0)
    state = jnp.einsum("htd,hte->hde", key_last, value, preferred_element_type=jnp.float32).astype(
        jnp.bfloat16
    )
    incoming = carried(state, flags, False)
    carry_in = jnp.where(continues, incoming, 0.0).astype(jnp.bfloat16)
    scores = jnp.einsum("htd,hsd->hts", query, key, preferred_element_type=jnp.float32)
    scores = jnp.where(same[None], scores, 0.0).astype(jnp.bfloat16)
    attended = jnp.einsum("hts,hsd->htd", scores, value, preferred_element_type=jnp.float32)
    attended = attended + jnp.einsum(
        "htd,hde->hte", query_first, carry_in, preferred_element_type=jnp.float32
    )
    attended = jnp.transpose(attended, (1, 0, 2)).reshape(count, local_width)
    squares = lax.psum(jnp.sum(attended * attended, axis=1), "tensor")
    rscale = lax.rsqrt(squares / (HEADS * HD) + epsilon)
    unit = attended * rscale[:, None]
    layer_out = (gain * unit).astype(jnp.bfloat16)
    upstream = grad_out[0].astype(jnp.float32)
    scaled = upstream * gain
    inner = lax.psum(jnp.sum(scaled * unit, axis=1), "tensor") / (HEADS * HD)
    grad_gain = lax.psum(jnp.sum(upstream * unit, axis=0), ("dp", "seq"))
    d_att = head_major(
        (rscale[:, None] * (scaled - unit * inner[:, None])).astype(jnp.bfloat16), shape
    )
    d_first = jnp.where(first_mask[None, :, None], d_att, 0)
    back_state = jnp.einsum(
        "htd,hte->hde", query_first, d_att, preferred_element_type=jnp.float32
    ).astype(jnp.bfloat16)
    outgoing = carried(back_state, flags, True)
    carry_back = jnp.where(last_block > block, outgoing, 0.0).astype(jnp.bfloat16)
    d_scores = jnp.einsum("hte,hse->hts", d_att, value, preferred_element_type=jnp.float32)
    d_scores = jnp.where(same[None], d_scores, 0.0).astype(jnp.bfloat16)
    grad_query = jnp.einsum("hts,hsd->htd", d_scores, key, preferred_element_type=jnp.float32)
    grad_query = grad_query + jnp.einsum(
        "hte,hde->htd", d_first, carry_in, preferred_element_type=jnp.float32
    )
    grad_key = jnp.einsum("hts,htd->hsd", d_scores, query, preferred_element_type=jnp.float32)
    grad_key = grad_key + jnp.einsum(
        "hse,hde->hsd", value_last, carry_back, preferred_element_type=jnp.float32
    )
    grad_value = jnp.einsum("hts,hte->hse", scores, d_att, preferred_element_type=jnp.float32)
    grad_value = grad_value + jnp.einsum(
        "hsd,hde->hse", key_last, carry_back, preferred_element_type=jnp.float32
    )
    out_shape = (1, count, local_width)

    def token_major(array):
        return jnp.transpose(array.astype(jnp.bfloat16), (1, 0, 2)).reshape(out_shape)

    return (
        layer_out.reshape(out_shape),
        token_major(grad_query),
        token_major(grad_key),
        token_major(grad_value),
        grad_gain,
    )


def solution(mesh):
    in_specs = (
        P("dp", "seq", "tensor"),
        P("dp", "seq", "tensor"),
        P("dp", "seq", "tensor"),
        P("dp", "seq", "tensor"),
        P("dp", None),
        P("tensor"),
    )
    out_specs = (
        P("dp", "seq", "tensor"),
        P("dp", "seq", "tensor"),
        P("dp", "seq", "tensor"),
        P("dp", "seq", "tensor"),
        P("tensor"),
    )
    return jax.shard_map(body, mesh=mesh, in_specs=in_specs, out_specs=out_specs, check_vma=False)
```

profile of v0, /device:TPU:0, one launch (start us, length us, event | category | flops | bytes accessed | tf_op | source)
XLA Modules:
  0.0 547.0 jit_solution(15308874766064887949)
XLA Ops:
  11.5 3.9 copy.79
  15.4 2.9 copy.82
  19.6 3.1 fusion.16
  24.8 69.2 %all-reduce = bf16[32]{0:T(256)(128)(2,1)S(1)} all-reduce(bf16[32]{0:T(256)(128)(2,1)S(1)} %dynamic-update-slice), channel_id=1, replica_groups=mesh['dp'=2,'seq'=32,'tensor'=2] {'seq'}, use_global_device_ids=true, to_apply=%add | all-reduce | flops 32 | bytes 128
  94.1 2.9 copy.78
  97.0 4.1 copy.87
  101.3 4.2 select_convert_fusion.1
  105.5 3.2 copy-done.1
  108.7 4.8 fusion.40
  113.6 5.0 fusion.7
  118.6 5.0 psum.21
  123.6 5.4 copy.88
  129.0 4.0 fusion.2
  133.0 5.1 psum.22
  138.2 4.3 fusion.8
  147.3 5.4 copy.86
  152.7 4.8 select_convert_fusion
  157.6 4.8 fusion.41
  162.4 4.3 add_convert_fusion.2
  166.7 3.9 copy.96
  170.6 252.2 %psum.23 = f32[2048]{0:T(1024)} all-reduce(f32[2048]{0:T(1024)S(1)} %get-tuple-element.155), channel_id=1, replica_groups=mesh['dp'=2,'seq'=32,'tensor'=2] {'dp','seq'}, use_global_device_ids=true, to_apply=%region_14.15 | all-reduce | flops 2048 | bytes 16384 | tf_op jit(solution)/shard_map/psum | solution.py:103
  422.8 3.9 multiply_convert_fusion
  426.7 6.7 %fusion.42 = f32[16,512,128]{1,2,0:T(8,128)} fusion(bf16[16,512,128]{1,2,0:T(8,128)(2,1)S(1)} %bitcast.105, bf16[16,512,512]{2,1,0:T(8,128)(2,1)} %copy-done), kind=kOutput, calls=%fused_computation.74 | convolution fusion | flops 1073741824 | bytes 14680064 | tf_op jit(solution)/shard_map/hts,htd->hsd/dot_general | solution.py:119
  433.5 86.6 %while.27 = (s32[]{:T(128)}, f32[16,128,128]{2,1,0:T(8,128)S(1)}, s32[]{:T(128)}, bf16[32,16,128,128]{3,2,1,0:T(8,128)(2,1)}, bf16[32,1]{0,1:T(2,128)(2,1)S(1)},...) while((s32[]{:T(128)}, f32[16,128,128]{2,1,0:T(8,128)S(1)}, s32[]{:T(128)}, ...), condition=%wide.region_12.13_spmd, body=%wide.region_11.12_spmd.sunk | while | flops 786439 | bytes 2621605 | solution.py:31
  434.2 2.1 convert_add_fusion.5
  437.0 2.1 convert_add_fusion.5
  439.8 2.1 convert_add_fusion.5
  442.6 2.1 convert_add_fusion.5
  445.4 2.1 convert_add_fusion.5
  448.1 2.1 convert_add_fusion.5
  450.9 2.1 convert_add_fusion.5
  453.7 2.1 convert_add_fusion.5
  456.5 2.1 convert_add_fusion.5
  459.3 2.1 convert_add_fusion.5
  462.1 2.1 convert_add_fusion.5
  464.9 2.1 convert_add_fusion.5
  467.7 2.1 convert_add_fusion.5
  470.4 2.1 convert_add_fusion.5
  473.2 2.1 convert_add_fusion.5
  476.0 2.1 convert_add_fusion.5
  478.8 2.1 convert_add_fusion.5
  481.6 2.1 convert_add_fusion.5
  484.4 2.1 convert_add_fusion.5
  487.2 2.1 convert_add_fusion.5
  521.8 6.2 %add_convert_fusion = bf16[16,512,128]{1,2,0:T(8,128)(2,1)} fusion(f32[16,512,128]{1,2,0:T(8,128)S(1)} %fusion.14, bf16[16,512,128]{1,2,0:T(8,128)(2,1)S(1)} %copy-done.9, bf16[16,512,512]{2,1,0:T(8,128)(2,1)} %copy-done.1), kind=kOutput, calls=%fused_computation.18 | convolution fusion | flops 1075838976 | bytes 16777216 | tf_op jit(solution)/shard_map/hts,hte->hse/dot_general | solution.py:123
  528.0 4.1 copy.98
  532.1 4.2 add_convert_fusion.1
  536.3 3.9 copy.97
  (93 shorter events, 56.2 us)
Async XLA Ops:
  7.2 106.3 %all-gather.5.cloned.1.call-start = ((), (), s32[]{:S(2)}) async-start(), calls=%async_computation | async-start | bytes 17301504 | tf_op jit(solution)/shard_map/all_gather | solution.py:16
  18.3 4.5 copy-start.2
  19.6 3.9 copy-start.11
  22.8 410.6 %all-gather.7.cloned.1.call-start = ((), (), s32[]{:S(2)}) async-start(), calls=%async_computation.1 | async-start | bytes 17301504 | tf_op jit(solution)/shard_map/all_gather | solution.py:16
  101.3 7.4 %copy-start.3 = (bf16[1,512,2048]{1,2,0:T(8,128)(2,1)S(1)}, bf16[1,512,2048]{1,2,0:T(8,128)(2,1)}, u32[]{:S(2)}) copy-start(bf16[1,512,2048]{1,2,0:T(8,128)(2,1)} %copy-done.2) | copy-start | bytes 6291460
  105.5 3.2 copy-start.1
  123.6 5.4 copy-start.10
  142.4 1.4 copy-start.7
  152.7 4.8 copy-start.5
  157.6 4.8 copy-start
  157.6 4.8 copy-start.8
  433.5 86.7 %copy-start.6 = (bf16[1,512,2048]{1,2,0:T(8,128)(2,1)S(1)}, bf16[1,512,2048]{1,2,0:T(8,128)(2,1)}, u32[]{:S(2)}) copy-start(bf16[1,512,2048]{1,2,0:T(8,128)(2,1)} %copy.79) | copy-start | bytes 6291460
  520.2 1.6 copy-start.9
  528.0 4.1 copy-start.4
Sparse Core Ops, SparseCore 0:
  22.9 75.2 all-gather.4
  145.5 151.3 all-gather.6
where the time goes:
time: 550 us; the launch traced here: 547 us
  blocking collectives  332 us (60%)
  other arithmetic  103 us (19%)
  matrix products  50.3 us (9%)
  local copies, waits for them, and re-layouts  44.8 us (8%)
  between operations  16.2 us (3%)
    psum x1, blocking collectives, body(): grad_gain = lax.psum(jnp.sum(upstream * unit, axis=0), ('dp', 'seq'))  252 us
    unnamed x1, blocking collectives  69.2 us
    add x31, other arithmetic, linked(): return (later[0] + keeping * earlier[0], jnp.maximum(earlier[1], later[1]))  65.4 us
    unnamed x33, local copies, waits for them, and re-layouts  28.3 us
    sub x31, other arithmetic, linked(): keeping = 1.0 - later[1][0]  20.3 us
  transfers between devices with their start and end apart: 2, of which 0 were waited for; matrix products, arithmetic and copies ran while one was open for 10% of the time, Pallas kernels for 0%

commit v1 on v0

--- a/solution.py
+++ b/solution.py
@@ -100,7 +100,8 @@
     upstream = grad_out[0].astype(jnp.float32)
     scaled = upstream * gain
     inner = lax.psum(jnp.sum(scaled * unit, axis=1), "tensor") / (HEADS * HD)
-    grad_gain = lax.psum(jnp.sum(upstream * unit, axis=0), ("dp", "seq"))
+    do_modes = lambda patch: lax.psum(lax.psum(patch, "seq"), "dp")
+    grad_gain = do_modes(jnp.sum(upstream * unit, axis=0))
     d_att = head_major(
         (rscale[:, None] * (scaled - unit * inner[:, None])).astype(jnp.bfloat16), shape
     )

time: 550 us -> 453 us (0.82)
  blocking collectives: 332 us -> 235 us
    psum x1 -> x2, blocking collectives: 252 us -> 156 us  [body(): do_modes = lambda patch: lax.psum(lax.psum(patch, 'seq'), 'dp')]
  transfers between devices with their start and end apart: 2 -> 2, of which waited for: 0 -> 0; matrix products, arithmetic and copies ran while one was open for 10% -> 12% of each run, Pallas kernels for 0% -> 0%
where the time goes in v1:
time: 453 us; the launch traced here: 450 us
  blocking collectives  235 us (52%)
  other arithmetic  103 us (23%)
  matrix products  50.4 us (11%)
  local copies, waits for them, and re-layouts  44.8 us (10%)
  between operations  16.2 us (4%)
    psum x2, blocking collectives, body(): do_modes = lambda patch: lax.psum(lax.psum(patch, 'seq'), 'dp')  156 us
    unnamed x1, blocking collectives  69.2 us
    add x31, other arithmetic, linked(): return (later[0] + keeping * earlier[0], jnp.maximum(earlier[1], later[1]))  65.4 us
    unnamed x33, local copies, waits for them, and re-layouts  28.3 us
    sub x31, other arithmetic, linked(): keeping = 1.0 - later[1][0]  20.3 us
    reshape x2, local copies, waits for them, and re-layouts, body(): attended = jnp.transpose(attended, (1, 0, 2)).reshape(count, local_width)  10.8 us
  transfers between devices with their start and end apart: 2, of which 0 were waited for; matrix products, arithmetic and copies ran while one was open for 12% of the time, Pallas kernels for 0%

profile of v1, /device:TPU:0, one launch (start us, length us, event | category | flops | bytes accessed | tf_op | source)
XLA Modules:
  0.0 450.4 jit_solution(10993581413240842437)
XLA Ops:
  11.5 3.9 copy.79
  15.4 2.9 copy.82
  19.6 3.1 fusion.16
  24.8 69.2 %all-reduce = bf16[32]{0:T(256)(128)(2,1)S(1)} all-reduce(bf16[32]{0:T(256)(128)(2,1)S(1)} %dynamic-update-slice), channel_id=1, replica_groups=mesh['dp'=2,'seq'=32,'tensor'=2] {'seq'}, use_global_device_ids=true, to_apply=%add | all-reduce | flops 32 | bytes 128
  94.1 2.9 copy.78
  97.0 4.1 copy.87
  101.3 4.2 select_convert_fusion.1
  105.5 3.2 copy-done.1
  108.7 4.8 %fusion.40 = f32[16,512,128]{1,2,0:T(8,128)} fusion(bf16[16,512,512]{2,1,0:T(8,128)(2,1)S(1)} %select_convert_fusion.1, bf16[16,512,128]{1,2,0:T(8,128)(2,1)S(1)} %bitcast.108), kind=kOutput, calls=%fused_computation.72 | convolution fusion | flops 1073741824 | bytes 14680064 | tf_op jit(solution)/shard_map/hts,hsd->htd/dot_general | solution.py:91
  113.6 5.0 %fusion.7 = (f32[512]{0:T(512)S(1)}, f32[16,512,128]{1,2,0:T(8,128)}) fusion(f32[16,512,128]{1,2,0:T(8,128)} %fusion.40, f32[16,128,128]{2,1,0:T(8,128)S(1)} %get-tuple-element.133, pred[]{:T(512)S(6)} %not.3, bf16[16,512,128]{1,2,0:T(8,128)(2,1)S(1)} %bitcast.103, pred[512]{0:T(512)(128)(4,1)S(1)} %get-tuple-element.180), kind=kOutput, calls=%fused_computation.17 | convolution fusion | flops 272891392 | bytes 11536897 | tf_op jit(solution)/shard_map/htd,hde->hte/dot_general | solution.py:92
  118.6 5.0 %psum.28 = f32[512]{0:T(512)S(1)} all-reduce(f32[512]{0:T(512)S(1)} %get-tuple-element.183), channel_id=1, replica_groups=mesh['dp'=2,'seq'=32,'tensor'=2] {'tensor'}, use_global_device_ids=true, to_apply=%region_7.8 | all-reduce | flops 512 | bytes 4096 | tf_op jit(solution)/shard_map/psum | solution.py:96
  123.6 5.4 %copy.88 = f32[512,2048]{1,0:T(8,128)} copy(f32[512,2048]{0,1:T(8,128)} %bitcast.100) | data formatting | bytes 8388608 | tf_op jit(solution)/shard_map/reshape | solution.py:95
  129.0 4.0 fusion.2
  133.0 5.1 %psum.29 = f32[512]{0:T(512)S(1)} all-reduce(f32[512]{0:T(512)S(1)} %get-tuple-element.156), channel_id=1, replica_groups=mesh['dp'=2,'seq'=32,'tensor'=2] {'tensor'}, use_global_device_ids=true, to_apply=%region_9.10 | all-reduce | flops 512 | bytes 4096 | tf_op jit(solution)/shard_map/psum | solution.py:102
  138.2 4.3 fusion.8
  147.3 5.4 %copy.86 = f32[1,512,2048]{2,1,0:T(8,128)} copy(f32[1,512,2048]{1,2,0:T(8,128)} %bitcast.101) | data formatting | bytes 8388608 | tf_op jit(solution)/shard_map/reshape | solution.py:95
  152.7 4.8 %select_convert_fusion = bf16[16,512,512]{2,1,0:T(8,128)(2,1)S(1)} fusion(bf16[16,512,128]{1,2,0:T(8,128)(2,1)} %copy-done.7, bf16[16,512,128]{1,2,0:T(8,128)(2,1)} %bitcast.107, pred[512,512]{1,0:T(8,128)(4,1)S(1)} %fusion.24), kind=kOutput, calls=%fused_computation.4 | convolution fusion | flops 1082130432 | bytes 12845056 | tf_op jit(solution)/shard_map/hte,hse->hts/dot_general | solution.py:114
  157.6 4.8 %fusion.41 = f32[16,512,128]{1,2,0:T(8,128)} fusion(bf16[16,512,512]{2,1,0:T(8,128)(2,1)S(1)} %select_convert_fusion, bf16[16,512,128]{1,2,0:T(8,128)(2,1)S(1)} %bitcast.112), kind=kOutput, calls=%fused_computation.73 | convolution fusion | flops 1073741824 | bytes 14680064 | tf_op jit(solution)/shard_map/hts,hsd->htd/dot_general | solution.py:116
  162.4 4.3 add_convert_fusion.2
  166.7 3.9 copy.96
  170.6 148.3 %psum.30 = f32[2048]{0:T(1024)S(1)} all-reduce(f32[2048]{0:T(1024)S(1)} %get-tuple-element.155), channel_id=1, replica_groups=mesh['dp'=2,'seq'=32,'tensor'=2] {'seq'}, use_global_device_ids=true, to_apply=%region_14.15 | all-reduce | flops 2048 | bytes 16384 | tf_op jit(solution)/shard_map/psum | solution.py:103
  318.9 7.2 %psum.31 = f32[2048]{0:T(1024)} all-reduce(f32[2048]{0:T(1024)S(1)} %psum.30), channel_id=1, replica_groups=mesh['dp'=2,'seq'=32,'tensor'=2] {'dp'}, use_global_device_ids=true, to_apply=%region_15.16 | all-reduce | flops 2048 | bytes 16384 | tf_op jit(solution)/shard_map/psum | solution.py:103
  326.1 3.9 multiply_convert_fusion
  330.0 6.7 %fusion.42 = f32[16,512,128]{1,2,0:T(8,128)} fusion(bf16[16,512,128]{1,2,0:T(8,128)(2,1)S(1)} %bitcast.105, bf16[16,512,512]{2,1,0:T(8,128)(2,1)} %copy-done), kind=kOutput, calls=%fused_computation.74 | convolution fusion | flops 1073741824 | bytes 14680064 | tf_op jit(solution)/shard_map/hts,htd->hsd/dot_general | solution.py:120
  336.8 86.6 %while.27 = (s32[]{:T(128)}, f32[16,128,128]{2,1,0:T(8,128)S(1)}, s32[]{:T(128)}, bf16[32,16,128,128]{3,2,1,0:T(8,128)(2,1)}, bf16[32,1]{0,1:T(2,128)(2,1)S(1)},...) while((s32[]{:T(128)}, f32[16,128,128]{2,1,0:T(8,128)S(1)}, s32[]{:T(128)}, ...), condition=%wide.region_12.13_spmd, body=%wide.region_11.12_spmd.sunk | while | flops 786439 | bytes 2621605 | solution.py:31
  337.5 2.1 convert_add_fusion.5
  340.3 2.1 convert_add_fusion.5
  343.1 2.1 convert_add_fusion.5
  345.9 2.1 convert_add_fusion.5
  348.7 2.1 convert_add_fusion.5
  351.5 2.1 convert_add_fusion.5
  354.2 2.1 convert_add_fusion.5
  357.0 2.1 convert_add_fusion.5
  359.8 2.1 convert_add_fusion.5
  362.6 2.1 convert_add_fusion.5
  365.4 2.1 convert_add_fusion.5
  368.2 2.1 convert_add_fusion.5
  371.0 2.1 convert_add_fusion.5
  373.8 2.1 convert_add_fusion.5
  376.5 2.1 convert_add_fusion.5
  379.3 2.1 convert_add_fusion.5
  382.1 2.1 convert_add_fusion.5
  384.9 2.1 convert_add_fusion.5
  387.7 2.1 convert_add_fusion.5
  425.1 6.2 %add_convert_fusion = bf16[16,512,128]{1,2,0:T(8,128)(2,1)} fusion(f32[16,512,128]{1,2,0:T(8,128)S(1)} %fusion.14, bf16[16,512,128]{1,2,0:T(8,128)(2,1)S(1)} %copy-done.9, bf16[16,512,512]{2,1,0:T(8,128)(2,1)} %copy-done.1), kind=kOutput, calls=%fused_computation.18 | convolution fusion | flops 1075838976 | bytes 16777216 | tf_op jit(solution)/shard_map/hts,hte->hse/dot_general | solution.py:124
  431.3 4.1 copy.98
  435.4 4.2 add_convert_fusion.1
  439.6 3.9 copy.97
  (94 shorter events, 58.3 us)
Async XLA Ops:
  7.2 106.3 %all-gather.5.cloned.1.call-start = ((), (), s32[]{:S(2)}) async-start(), calls=%async_computation | async-start | bytes 17301504 | tf_op jit(solution)/shard_map/all_gather | solution.py:16
  18.3 4.5 copy-start.2
  19.6 3.9 copy-start.11
  22.8 314.0 %all-gather.7.cloned.1.call-start = ((), (), s32[]{:S(2)}) async-start(), calls=%async_computation.1 | async-start | bytes 17301504 | tf_op jit(solution)/shard_map/all_gather | solution.py:16
  101.3 7.4 %copy-start.3 = (bf16[1,512,2048]{1,2,0:T(8,128)(2,1)S(1)}, bf16[1,512,2048]{1,2,0:T(8,128)(2,1)}, u32[]{:S(2)}) copy-start(bf16[1,512,2048]{1,2,0:T(8,128)(2,1)} %copy-done.2) | copy-start | bytes 6291460
  105.5 3.2 copy-start.1
  123.6 5.4 %copy-start.10 = (f32[2048]{0:T(1024)S(1)}, f32[2048]{0:T(1024)}, u32[]{:S(2)}) copy-start(f32[2048]{0:T(1024)} %param.15) | copy-start | bytes 24580
  142.4 1.4 copy-start.7
  152.7 4.8 %copy-start.5 = (bf16[1,512,2048]{1,2,0:T(8,128)(2,1)S(1)}, bf16[1,512,2048]{1,2,0:T(8,128)(2,1)}, u32[]{:S(2)}) copy-start(bf16[1,512,2048]{1,2,0:T(8,128)(2,1)} %copy.79) | copy-start | bytes 6291460
  157.6 4.8 %copy-start = (bf16[16,512,512]{2,1,0:T(8,128)(2,1)}, bf16[16,512,512]{2,1,0:T(8,128)(2,1)S(1)}, u32[]{:S(2)}) copy-start(bf16[16,512,512]{2,1,0:T(8,128)(2,1)S(1)} %select_convert_fusion) | copy-start | bytes 25165828
  157.6 4.8 %copy-start.8 = (bf16[16,512,128]{1,2,0:T(8,128)(2,1)S(1)}, bf16[16,512,128]{1,2,0:T(8,128)(2,1)}, u32[]{:S(2)}) copy-start(bf16[16,512,128]{1,2,0:T(8,128)(2,1)} %copy-done.7) | copy-start | bytes 6291460
  336.8 86.7 %copy-start.6 = (bf16[1,512,2048]{1,2,0:T(8,128)(2,1)S(1)}, bf16[1,512,2048]{1,2,0:T(8,128)(2,1)}, u32[]{:S(2)}) copy-start(bf16[1,512,2048]{1,2,0:T(8,128)(2,1)} %copy.79) | copy-start | bytes 6291460
  423.5 1.6 copy-start.9
  431.3 4.1 copy-start.4
Sparse Core Ops, SparseCore 0:
  22.9 75.2 all-gather.4
  145.5 151.4 all-gather.6
